TPU v7x, 256 devices: a whole 4x4x8 slice. The times are simulated.
256 devices in a mesh: ref: 64 (over z, y_lo, x), win: 4 (over y_hi, core).
Axes of the slice: x: 4, y: 4 (y_hi: 2, y_lo: 2; y = y_hi * 2 + y_lo), z: 8, core: 2. Of those that a mesh axis runs over, the one named last changes fastest.
Arguments:
- queries: bfloat16 [2048, 8192], P('ref', 'win'), may hold values from -1 to 1, as said below
- references: bfloat16 [65536, 8192], P('ref', 'win'), may hold values from -1 to 1, as said below
- labels: int32 [512], P('ref'), may hold values from 0 to 7, as said below
- kernel: float32 [9, 8], replicated, may hold values from 0.02 to 0.3
- class_bias: float32 [8], replicated, may hold values from -4 to 4
Outputs:
- ancestry_logprob: float32 [16, 8, 2048], P('win', None, 'ref')
Inputs may be any that keep to these rules, and one draw needn't show every extreme that they name: `queries`: every entry is -1 or +1. `references`: every entry is -1 or +1. Every ancestry labels at least one block.
All inputs are finite; a program needn't handle non-finite values.
Results may differ from a plain program's by a relative error of at most 0.0003.
Values may be sent and summed in bfloat16 or wider, within the bound.
A program may use at most 64 MiB of HBM per device.

v0:
```python
import jax
import jax.numpy as jnp
from jax import lax
from jax.sharding import PartitionSpec as P

S = 512
A = 8
BLOCK = 128
TAPS = 9
neg_floor = -1e30


def combined_all(shard, axis, combine):
    everything = lax.all_gather(shard, axis)
    leading = everything[0]

    def lap(k, so_far):
        return combine(so_far, everything[k])

    return lax.fori_loop(1, lax.axis_size(axis), lap, leading)


def with_halo(block, sides, width):
    for axis, dim in sides:
        count = lax.axis_size(axis)
        forward = [(i, i + 1) for i in range(count - 1)]
        backward = [(target, source) for source, target in forward]
        low = lax.ppermute(
            lax.slice_in_dim(block, block.shape[dim] - width, None, axis=dim), axis, forward
        )
        high = lax.ppermute(lax.slice_in_dim(block, 0, width, axis=dim), axis, backward)
        block = jnp.concatenate([low, block, high], axis=dim)
    return block


def pool_rows(query_piece, references, member, windows):
    score_scale = 256.0 / S
    row_count = query_piece.shape[0]
    block_count = references.shape[0] // BLOCK
    results = []
    for window in range(windows):
        query_part = query_piece[:, window * S : (window + 1) * S]
        ref_part = references[:, window * S : (window + 1) * S]
        scores = (
            jnp.einsum("qs,rs->qr", query_part, ref_part, preferred_element_type=jnp.float32)
            * score_scale
        )
        blocks = scores.reshape(row_count, block_count, BLOCK)
        block_peak = jnp.max(blocks, axis=2)
        block_total = jnp.sum(jnp.exp(blocks - block_peak[:, :, None]), axis=2)
        group_peak = jnp.max(jnp.where(member[None], block_peak[:, :, None], neg_floor), axis=1)
        weights = jnp.where(
            member[None],
            block_total[:, :, None] * jnp.exp(block_peak[:, :, None] - group_peak[:, None, :]),
            0.0,
        )
        group_total = jnp.sum(weights, axis=1)
        group_lse = jnp.where(group_total > 0, group_peak + jnp.log(group_total), neg_floor)
        results.append(group_lse.T)
    return jnp.stack(results)


def combine_lse(left_part, right_part):
    higher = jnp.maximum(left_part, right_part)
    return higher + jnp.log(jnp.exp(left_part - higher) + jnp.exp(right_part - higher))


def per_device(queries, references, labels, kernel, class_bias):
    member = labels[:, None] == jnp.arange(A, dtype=jnp.int32)[None, :]
    windows = references.shape[1] // S
    query_count = queries.shape[0]
    partial_value = pool_rows(
        lax.all_gather(queries, "ref", axis=0, tiled=True), references, member, windows
    )
    owner_start = lax.axis_index("ref") * query_count
    combined = combined_all(partial_value, "ref", combine_lse)
    pooled = lax.dynamic_slice_in_dim(combined, owner_start, query_count, 2)
    centered = pooled - jnp.mean(pooled, axis=1, keepdims=True)
    padded = with_halo(centered, (("win", 0),), TAPS // 2)
    smoothed = jnp.zeros_like(centered)
    for offset in range(TAPS):
        smoothed = smoothed + kernel[offset][None, :, None] * padded[offset : offset + windows]
    logits = smoothed + class_bias[None, :, None]
    return jax.nn.log_softmax(logits, axis=1)


def solution(mesh):
    in_specs = (P("ref", "win"), P("ref", "win"), P("ref"), P(), P())
    out_specs = P("win", None, "ref")
    return jax.shard_map(
        per_device, mesh=mesh, in_specs=in_specs, out_specs=out_specs, check_vma=False
    )
```

profile of v0, /device:TPU:1, one launch (start us, length us, event | category | flops | bytes accessed | tf_op | source)
XLA Modules:
  0.0 761.7 jit_solution(14383319232930999667)
XLA Ops:
  8.0 274.8 %all-gather.4.cloned.1.call-done = bf16[2048,2048]{1,0:T(8,128)(2,1)} async-done(((bf16[32,2048]{1,0:T(8,128)(2,1)}), bf16[2048,2048]{1,0:T(8,128)(2,1)}) %all-gather.4.cloned.1.call-update) | async-done | bytes 8388624 | tf_op jit(solution)/shard_map/all_gather | solution.py:73
  282.9 4.4 bitcast_reduce_fusion.3
  287.3 1.5 fusion.15
  288.9 1.8 copy-done.1
  290.7 2.4 bitcast_reduce_fusion
  293.1 1.5 fusion.9
  294.6 2.4 bitcast_reduce_fusion.1
  297.0 1.5 fusion.11
  298.5 2.6 bitcast_reduce_fusion.2
  301.1 1.5 fusion.13
  304.1 325.6 %all-gather.6.cloned.1.call-done = f32[256,8,2048]{2,1,0:T(8,128)} async-done(((f32[4,8,2048]{2,1,0:T(8,128)}), f32[256,8,2048]{2,1,0:T(8,128)}) %all-gather.6.cloned.1.call-update) | async-done | bytes 16777232 | tf_op jit(solution)/shard_map/all_gather | solution.py:14
  630.6 76.0 %while.15 = (s32[]{:T(128)}, f32[4,8,2048]{2,1,0:T(8,128)S(1)}, f32[64,4,8,2048]{3,2,1,0:T(8,128)}, s32[]{:T(128)}, s32[]{:T(128)}, /*index=5*/s32[]{:T(128)}) while((s32[]{:T(128)}, f32[4,8,2048]{2,1,0:T(8,128)S(1)}, f32[64,4,8,2048]{3,2,1,0:T(8,128)}, s32[]{:T(128)}, s32[]{:T(128)}, /*index=5*/s32[]{:T(128)}) %tuple.62), condition=%wide.region_17.18_spmd, body=%wide.region_16.17_spmd.sunk | while | flops 327685 | bytes 786539 | solution.py:20
  630.6 1.2 fusion.53
  631.8 1.2 fusion.53
  633.0 1.2 fusion.53
  634.2 1.2 fusion.53
  635.4 1.2 fusion.53
  636.6 1.2 fusion.53
  637.8 1.2 fusion.53
  639.0 1.2 fusion.53
  640.2 1.2 fusion.53
  641.4 1.2 fusion.53
  642.7 1.2 fusion.53
  643.9 1.2 fusion.53
  645.1 1.2 fusion.53
  646.3 1.2 fusion.53
  647.5 1.2 fusion.53
  648.7 1.2 fusion.53
  649.9 1.2 fusion.53
  651.1 1.2 fusion.53
  652.3 1.2 fusion.53
  653.5 1.2 fusion.53
  654.7 1.2 fusion.53
  655.9 1.2 fusion.53
  657.1 1.2 fusion.53
  658.3 1.2 fusion.53
  659.5 1.2 fusion.53
  660.7 1.2 fusion.53
  661.9 1.2 fusion.53
  663.2 1.2 fusion.53
  664.4 1.2 fusion.53
  665.6 1.2 fusion.53
  666.8 1.2 fusion.53
  668.0 1.2 fusion.53
  669.2 1.2 fusion.53
  670.4 1.2 fusion.53
  671.6 1.2 fusion.53
  672.8 1.2 fusion.53
  674.0 1.2 fusion.53
  675.2 1.2 fusion.53
  676.4 1.2 fusion.53
  678.8 1.2 fusion.53
  681.2 1.2 fusion.53
  683.6 1.2 fusion.53
  686.1 1.2 fusion.53
  688.5 1.2 fusion.53
  690.9 1.2 fusion.53
  693.3 1.2 fusion.53
  695.7 1.2 fusion.53
  699.3 1.2 fusion.53
  701.7 1.2 fusion.53
  704.1 1.2 fusion.53
  706.7 42.3 %collective-permute-start.1 = (f32[4,8,32]{2,1,0:T(8,128)S(1)}, f32[4,8,32]{2,1,0:T(8,128)S(1)}, u32[]{:S(2)}, u32[]{:S(2)}) collective-permute-start(f32[4,8,32]{2,1,0:T(8,128)S(1)} %dynamic-slice_subtract_fusion), channel_id=1, source_target_pairs={{1,0},{2,1},{3,2},{5,4},{6,5},{7,6},{9,8},{10,9},{11,10},{13,12},{... | collective-permute-start | bytes 12296 | tf_op jit(solution)/shard_map/ppermute | solution.py:31
  749.0 4.3 collective-permute-start
  (40 shorter events, 21.2 us)
Async XLA Ops:
  6.5 276.3 %all-gather.4.cloned.1.call-start = ((), (), s32[]{:S(2)}) async-start(), calls=%async_computation | async-start | bytes 8519680 | tf_op jit(solution)/shard_map/all_gather | solution.py:73
  7.3 622.4 %all-gather.6.cloned.1.call-start = ((), (), s32[]{:S(2)}) async-start(), calls=%async_computation.1 | async-start | bytes 17039360 | tf_op jit(solution)/shard_map/all_gather | solution.py:14
  282.9 6.0 copy-start.2
  287.3 3.4 copy-start.1
  301.1 452.2 %copy-start = (f32[9,8]{0,1:T(8,128)S(1)}, f32[9,8]{0,1:T(8,128)}, u32[]{:S(2)}) copy-start(f32[9,8]{0,1:T(8,128)} %param.10) | copy-start | bytes 868
  301.1 453.1 %copy-start.3 = (f32[8]{0:T(128)S(1)}, f32[8]{0:T(128)}, u32[]{:S(2)}) copy-start(f32[8]{0:T(128)} %param.11) | copy-start | bytes 100
  706.7 46.9 %collective-permute-start.1 = (f32[4,8,32]{2,1,0:T(8,128)S(1)}, f32[4,8,32]{2,1,0:T(8,128)S(1)}, u32[]{:S(2)}, u32[]{:S(2)}) collective-permute-start(f32[4,8,32]{2,1,0:T(8,128)S(1)} %dynamic-slice_subtract_fusion), channel_id=1, source_target_pairs={{1,0},{2,1},{3,2},{5,4},{6,5},{7,6},{9,8},{10,9},{11,10},{13,12},{... | collective-permute-start | bytes 12296 | tf_op jit(solution)/shard_map/ppermute | solution.py:31
  749.0 5.2 collective-permute-start
Sparse Core Ops, SparseCore 0:
  9.1 273.7 all-gather.3
  304.2 325.3 all-gather.5
where the time goes:
time: 764 us; the launch traced here: 762 us
  waiting for transfers between devices  602 us (79%)
  other arithmetic  83.8 us (11%)
  starting transfers between devices  46.6 us (6%)
  between operations  13.6 us (2%)
  matrix products  11.8 us (2%)
    all_gather x1, waiting for transfers between devices, combined_all(): everything = lax.all_gather(shard, axis)  326 us
    all_gather x1, waiting for transfers between devices, per_device(): lax.all_gather(queries, 'ref', axis=0, tiled=True)  275 us
    add x63, other arithmetic, combine_lse(): higher + jnp.log(jnp.exp(left_part - higher) + jnp.exp(right_part - higher))  74.7 us
    ppermute x1, starting transfers between devices, with_halo(): lax.ppermute(lax.slice_in_dim(block, 0, width, axis=dim), axis, backward)  42.3 us
  transfers between devices with their start and end apart: 4, of which 3 were waited for; matrix products, arithmetic and copies ran while one was open for 0% of the time, Pallas kernels for 0%

commit v1 on v0

--- a/solution.py
+++ b/solution.py
@@ -1,3 +1,4 @@
+import functools
 import jax
 import jax.numpy as jnp
 from jax import lax
@@ -8,6 +9,17 @@
 BLOCK = 128
 TAPS = 9
 neg_floor = -1e30
+
+
+def windows_measure(local_array, across):
+    y2 = jnp.concatenate(
+        lax.all_to_all(jnp.stack(lax.axis_size(across) * [local_array], axis=0), across, 0, 0),
+        axis=0,
+    )
+    return y2
+
+
+attach_slot_for = functools.partial(windows_measure, across="ref")
 
 
 def combined_all(shard, axis, combine):
@@ -69,9 +81,7 @@
     member = labels[:, None] == jnp.arange(A, dtype=jnp.int32)[None, :]
     windows = references.shape[1] // S
     query_count = queries.shape[0]
-    partial_value = pool_rows(
-        lax.all_gather(queries, "ref", axis=0, tiled=True), references, member, windows
-    )
+    partial_value = pool_rows(attach_slot_for(queries), references, member, windows)
     owner_start = lax.axis_index("ref") * query_count
     combined = combined_all(partial_value, "ref", combine_lse)
     pooled = lax.dynamic_slice_in_dim(combined, owner_start, query_count, 2)

time: 764 us -> 661 us (0.87)
  waiting for transfers between devices: 602 us -> 471 us
  starting transfers between devices: 46.6 us -> 60.5 us
  matrix products: 11.8 us -> 19.6 us
    all_gather x1 -> x0, waiting for transfers between devices: 275 us -> none  [per_device(): lax.all_gather(queries, 'ref', axis=0, tiled=True)]
    all_to_all x0 -> x1, waiting for transfers between devices: none -> 181 us  [windows_measure(): lax.all_to_all(jnp.stack(lax.axis_size(across) * [local_array], axis=0),...]
    all_gather x1, waiting for transfers between devices: 326 us -> 289 us  [combined_all(): everything = lax.all_gather(shard, axis)]
    all_to_all x0 -> x1, starting transfers between devices: none -> 13.9 us  [windows_measure(): lax.all_to_all(jnp.stack(lax.axis_size(across) * [local_array], axis=0),...]
    dot_general x4, matrix products: 11.8 us -> 19.6 us  [pool_rows(): jnp.einsum('qs,rs->qr', query_part, ref_part, preferred_element_type=jnp....]
where the time goes in v1:
time: 661 us; the launch traced here: 659 us
  waiting for transfers between devices  471 us (71%)
  other arithmetic  86.7 us (13%)
  starting transfers between devices  60.5 us (9%)
  matrix products  19.6 us (3%)
  between operations  13.6 us (2%)
    all_gather x1, waiting for transfers between devices, combined_all(): everything = lax.all_gather(shard, axis)  289 us
    all_to_all x1, waiting for transfers between devices, windows_measure(): lax.all_to_all(jnp.stack(lax.axis_size(across) * [local_array], axis=0),...  181 us
    add x63, other arithmetic, combine_lse(): higher + jnp.log(jnp.exp(left_part - higher) + jnp.exp(right_part - higher))  74.7 us
    ppermute x1, starting transfers between devices, with_halo(): lax.ppermute(lax.slice_in_dim(block, 0, width, axis=dim), axis, backward)  42.3 us
    dot_general x4, matrix products, pool_rows(): jnp.einsum('qs,rs->qr', query_part, ref_part, preferred_element_type=jnp....  19.6 us
    all_to_all x1, starting transfers between devices, windows_measure(): lax.all_to_all(jnp.stack(lax.axis_size(across) * [local_array], axis=0),...  13.9 us
  transfers between devices with their start and end apart: 4, of which 3 were waited for; matrix products, arithmetic and copies ran while one was open for 0% of the time, Pallas kernels for 0%

profile of v1, /device:TPU:1, one launch (start us, length us, event | category | flops | bytes accessed | tf_op | source)
XLA Modules:
  0.0 658.7 jit_solution(13051394845209485029)
XLA Ops:
  6.5 5.2 stack.12
  11.7 13.9 %all-to-all-start = ((bf16[64,32,2048]{2,1,0:T(8,128)(2,1)}), bf16[64,32,2048]{2,1,0:T(8,128)(2,1)}, u32[]{:S(2)}, u32[]{:S(2)}) async-start(bf16[64,32,2048]{2,1,0:T(8,128)(2,1)} %stack.12), calls=%async_computation | async-start | bytes 16777216 | tf_op jit(solution)/shard_map/all_to_all | solution.py:16
  25.7 181.0 %all-to-all-done = bf16[64,32,2048]{2,1,0:T(8,128)(2,1)} async-done(((bf16[64,32,2048]{2,1,0:T(8,128)(2,1)}), bf16[64,32,2048]{2,1,0:T(8,128)(2,1)}, u32[]{:S(2)}, u32[]{:S(2)}) %all-to-all-start) | async-done | bytes 8388640 | tf_op jit(solution)/shard_map/all_to_all | solution.py:16
  206.7 4.4 bitcast_reduce_fusion
  211.1 4.0 bitcast_reduce_fusion.1
  215.1 4.0 bitcast_reduce_fusion.2
  219.1 7.2 %bitcast_reduce_fusion.3 = (f32[2048,8]{0,1:T(8,128)S(1)}, f32[2048,1024]{0,1:T(8,128)}) fusion(bf16[1024,2048]{1,0:T(8,128)(2,1)S(1)} %copy-done.1, bf16[2048,2048]{1,0:T(8,128)(2,1)} %bitcast.1), kind=kOutput, calls=%fused_computation.23 | convolution fusion | flops 2151661568 | bytes 11599872 | tf_op jit(solution)/shard_map/qs,rs->qr/dot_general | solution.py:57
  226.3 4.8 fusion.15
  231.3 1.5 fusion.9
  232.8 1.7 fusion.11
  234.5 1.5 fusion.13
  237.4 289.2 %all-gather.3.cloned.1.call-done = f32[256,8,2048]{2,1,0:T(8,128)} async-done(((f32[4,8,2048]{2,1,0:T(8,128)}), f32[256,8,2048]{2,1,0:T(8,128)}) %all-gather.3.cloned.1.call-update) | async-done | bytes 16777232 | tf_op jit(solution)/shard_map/all_gather | solution.py:26
  527.6 76.0 %while.15 = (s32[]{:T(128)}, f32[4,8,2048]{2,1,0:T(8,128)S(1)}, f32[64,4,8,2048]{3,2,1,0:T(8,128)}, s32[]{:T(128)}, s32[]{:T(128)}, /*index=5*/s32[]{:T(128)}) while((s32[]{:T(128)}, f32[4,8,2048]{2,1,0:T(8,128)S(1)}, f32[64,4,8,2048]{3,2,1,0:T(8,128)}, s32[]{:T(128)}, s32[]{:T(128)}, /*index=5*/s32[]{:T(128)}) %tuple.60), condition=%wide.region_17.18_spmd, body=%wide.region_16.17_spmd.sunk | while | flops 327685 | bytes 786539 | solution.py:32
  527.6 1.2 fusion.53
  528.8 1.2 fusion.53
  530.0 1.2 fusion.53
  531.2 1.2 fusion.53
  532.4 1.2 fusion.53
  533.6 1.2 fusion.53
  534.8 1.2 fusion.53
  536.0 1.2 fusion.53
  537.2 1.2 fusion.53
  538.4 1.2 fusion.53
  539.6 1.2 fusion.53
  540.9 1.2 fusion.53
  542.1 1.2 fusion.53
  543.3 1.2 fusion.53
  544.5 1.2 fusion.53
  545.7 1.2 fusion.53
  546.9 1.2 fusion.53
  548.1 1.2 fusion.53
  549.3 1.2 fusion.53
  550.5 1.2 fusion.53
  551.7 1.2 fusion.53
  552.9 1.2 fusion.53
  554.1 1.2 fusion.53
  555.3 1.2 fusion.53
  556.5 1.2 fusion.53
  557.7 1.2 fusion.53
  558.9 1.2 fusion.53
  560.1 1.2 fusion.53
  561.3 1.2 fusion.53
  562.6 1.2 fusion.53
  563.8 1.2 fusion.53
  565.0 1.2 fusion.53
  566.2 1.2 fusion.53
  567.4 1.2 fusion.53
  568.6 1.2 fusion.53
  569.8 1.2 fusion.53
  571.0 1.2 fusion.53
  573.4 1.2 fusion.53
  575.8 1.2 fusion.53
  578.2 1.2 fusion.53
  580.6 1.2 fusion.53
  583.1 1.2 fusion.53
  585.5 1.2 fusion.53
  587.9 1.2 fusion.53
  590.3 1.2 fusion.53
  593.9 1.2 fusion.53
  596.3 1.2 fusion.53
  598.7 1.2 fusion.53
  601.1 1.2 fusion.53
  603.7 42.3 %collective-permute-start.1 = (f32[4,8,32]{2,1,0:T(8,128)S(1)}, f32[4,8,32]{2,1,0:T(8,128)S(1)}, u32[]{:S(2)}, u32[]{:S(2)}) collective-permute-start(f32[4,8,32]{2,1,0:T(8,128)S(1)} %dynamic-slice_subtract_fusion), channel_id=1, source_target_pairs={{1,0},{2,1},{3,2},{5,4},{6,5},{7,6},{9,8},{10,9},{11,10},{13,12},{... | collective-permute-start | bytes 12296 | tf_op jit(solution)/shard_map/ppermute | solution.py:43
  646.0 4.3 collective-permute-start
  (40 shorter events, 21.0 us)
Async XLA Ops:
  11.7 13.9 %copy-start.2 = (s32[8]{0:T(128)S(1)}, s32[8]{0:T(128)}, u32[]{:S(2)}) copy-start(s32[8]{0:T(128)} %param.9) | copy-start | bytes 100
  11.7 195.0 %all-to-all-start = ((bf16[64,32,2048]{2,1,0:T(8,128)(2,1)}), bf16[64,32,2048]{2,1,0:T(8,128)(2,1)}, u32[]{:S(2)}, u32[]{:S(2)}) async-start(bf16[64,32,2048]{2,1,0:T(8,128)(2,1)} %stack.12), calls=%async_computation | async-start | bytes 16777216 | tf_op jit(solution)/shard_map/all_to_all | solution.py:16
  25.6 501.0 %all-gather.3.cloned.1.call-start = ((), (), s32[]{:S(2)}) async-start(), calls=%async_computation.1 | async-start | bytes 17039360 | tf_op jit(solution)/shard_map/all_gather | solution.py:26
  206.7 4.4 copy-start.1
  234.5 415.9 %copy-start = (f32[9,8]{0,1:T(8,128)S(1)}, f32[9,8]{0,1:T(8,128)}, u32[]{:S(2)}) copy-start(f32[9,8]{0,1:T(8,128)} %param.10) | copy-start | bytes 868
  234.5 416.7 %copy-start.3 = (f32[8]{0:T(128)S(1)}, f32[8]{0:T(128)}, u32[]{:S(2)}) copy-start(f32[8]{0:T(128)} %param.11) | copy-start | bytes 100
  603.7 46.9 %collective-permute-start.1 = (f32[4,8,32]{2,1,0:T(8,128)S(1)}, f32[4,8,32]{2,1,0:T(8,128)S(1)}, u32[]{:S(2)}, u32[]{:S(2)}) collective-permute-start(f32[4,8,32]{2,1,0:T(8,128)S(1)} %dynamic-slice_subtract_fusion), channel_id=1, source_target_pairs={{1,0},{2,1},{3,2},{5,4},{6,5},{7,6},{9,8},{10,9},{11,10},{13,12},{... | collective-permute-start | bytes 12296 | tf_op jit(solution)/shard_map/ppermute | solution.py:43
  646.0 5.2 collective-permute-start
Sparse Core Ops, SparseCore 0:
  237.6 288.9 all-gather.2
